TPU v7x, 256 devices: a whole 4x4x8 slice. The times are simulated.
256 devices in a mesh: ew: 8 (over y, z_hi), ns: 32 (over z_lo, x, core).
Axes of the slice: x: 4, y: 4, z: 8 (z_hi: 2, z_lo: 4; z = z_hi * 4 + z_lo), core: 2. Of those that a mesh axis runs over, the one named last changes fastest.
Arguments:
- couplings: bfloat16 [8, 32, 16, 128, 2048], P('ew', 'ns'), may hold values from -0.125 to 0.125
- inverses: bfloat16 [8, 32, 16, 128, 128], P('ew', 'ns'), as said below
- pattern: int32 [8, 32, 16, 16], P('ew', 'ns'), may hold values 0 or 1
- counts: int32 [8, 32], P('ew', 'ns'), may hold values from 1 to 16, as said below
- basis: bfloat16 [8, 32, 128, 2048], P('ew', 'ns'), may hold values from -0.125 to 0.125
Outputs:
- south_front: float32 [8, 32, 768, 768], P('ew', 'ns')
- west_front: float32 [8, 32, 256, 256], P('ew', 'ns')
- coarse: float32 [8, 32, 128, 128], P('ew', 'ns')
Inputs may be any that keep to these rules, and one draw needn't show every extreme that they name: `counts`: some subdomain has exactly 16 live block columns. `inverses`: each block is symmetric.
All inputs are finite; a program needn't handle non-finite values. No bound on the sum of `pattern` on one device may be relied on, other than what follows from the above.
Results may differ from a plain program's by a relative error of at most 0.0015.
Values may be sent and summed in bfloat16 or wider, within the bound.
No kernel may reach another device: no remote copies, remote signals or barrier semaphores. Data moves between devices by JAX's collectives and lax.ppermute only.
A program may use at most 128 MiB of HBM per device.

v0:
```python
import jax
import jax.numpy as jnp
from jax import lax
from jax.sharding import PartitionSpec as P

B = 128
SN = 6
SE = 2


def from_behind(block, axis, distance):
    devices = range(lax.axis_size(axis))
    route = [(i - distance, i) for i in devices if i - distance in devices]
    return lax.ppermute(block, axis, route)


def solve_all(slabs, inverse):
    return jnp.einsum("kab,kbc->kac", inverse, slabs, preferred_element_type=jnp.float32).astype(
        jnp.bfloat16
    )


def edge_parts(slabs, solved, edges):
    results = []
    for edge in edges:
        slab = slabs[:, :, edge[0] : edge[0] + edge[1]]
        answer = solved[:, :, edge[0] : edge[0] + edge[1]]
        results.append(-jnp.einsum("kbi,kbj->ij", slab, answer, preferred_element_type=jnp.float32))
    return tuple(results)


def pass_edges(high_parts):
    from_west = from_behind(high_parts[0], "ew", 1)
    from_south = from_behind(high_parts[1], "ns", 1)
    return (from_west, from_south)


def shards(couplings, inverses, pattern, counts, basis):
    coupling = couplings[0, 0]
    inverse = inverses[0, 0]
    touched = pattern[0, 0]
    count = counts[0, 0]
    blocks_total = coupling.shape[0]
    north_start = SN * B
    west_start = 2 * SN * B
    east_start = west_start + SE * B
    south_edge = (0, SN * B)
    north_edge = (north_start, SN * B)
    west_edge = (west_start, SE * B)
    east_edge = (east_start, SE * B)
    columns = jnp.repeat(touched, B, axis=1)
    live = (jnp.arange(blocks_total, dtype=jnp.int32) < count).astype(jnp.int32)[:, None]
    keep = (columns * live).astype(jnp.bfloat16)
    masked = coupling * keep[:, None, :]
    high_edges = [east_edge, north_edge]
    solved = solve_all(masked, inverse)
    every_part = edge_parts(masked, solved, [south_edge, west_edge] + high_edges)
    low_parts = every_part[:2]
    from_west, from_south = pass_edges(every_part[2:])
    south_front = low_parts[0] + from_south
    west_front = low_parts[1] + from_west
    front_half = west_front.astype(jnp.bfloat16)
    row_basis = basis[0, 0]
    rank = row_basis.shape[0]
    edge_width = SE * B
    piece = lax.all_gather(front_half, "ew", axis=0, tiled=True)
    pieces = piece.shape[0] // edge_width
    columns_here = row_basis.reshape(rank, pieces, edge_width)
    fronts = piece.reshape(pieces, edge_width, edge_width)
    projected = jnp.einsum(
        "rnk,nkl->rnl", columns_here, fronts, preferred_element_type=jnp.float32
    ).astype(jnp.bfloat16)
    coarse = jnp.einsum("rnl,snl->rs", projected, columns_here, preferred_element_type=jnp.float32)
    return (south_front[None, None], west_front[None, None], coarse[None, None])


def solution(mesh):
    return jax.shard_map(
        shards,
        mesh=mesh,
        in_specs=(
            P("ew", "ns", None, None, None),
            P("ew", "ns", None, None, None),
            P("ew", "ns", None, None),
            P("ew", "ns"),
            P("ew", "ns", None, None),
        ),
        out_specs=(P("ew", "ns", None, None), P("ew", "ns", None, None), P("ew", "ns", None, None)),
        check_vma=False,
    )
```

profile of v0, /device:TPU:2, one launch (start us, length us, event | category | flops | bytes accessed | tf_op | source)
XLA Modules:
  0.0 137.7 jit_solution(6369991985110612012)
XLA Ops:
  7.2 0.0 copy-start
  7.2 0.0 copy-start.3
  7.2 0.0 all-gather.2.cloned.1.call-start
  7.2 12.3 %copy.8 = bf16[1,1,16,128,2048]{3,4,2,1,0:T(8,128)(2,1)} copy(bf16[1,1,16,128,2048]{4,3,2,1,0:T(8,128)(2,1)} %param.5) | data formatting | bytes 16777216 | tf_op args[0]
  20.2 0.0 copy-done.3
  20.3 0.1 broadcast_in_dim.14
  20.4 0.1 fusion.29
  20.4 6.4 %bitcast_multiply_fusion = bf16[16,128,2048]{1,2,0:T(8,128)(2,1)S(1)} fusion(bf16[1,1,16,128,2048]{3,4,2,1,0:T(8,128)(2,1)} %copy.8, bf16[16,2048]{1,0:T(8,128)(2,1)S(1)} %fusion.29), kind=kLoop, calls=%fused_computation | loop fusion | flops 4194304 | bytes 16842752 | tf_op jit(solution)/shard_map/mul | solution.py:54
  26.8 0.0 copy-done
  26.8 0.0 copy-start.1
  26.8 5.1 %convert_bitcast_fusion = bf16[16,128,2048]{1,2,0:T(8,128)(2,1)} fusion(bf16[16,128,2048]{1,2,0:T(8,128)(2,1)S(1)} %bitcast_multiply_fusion, bf16[1,1,16,128,128]{4,3,2,1,0:T(8,128)(2,1)S(1)} %copy-done), kind=kOutput, calls=%fused_computation.1 | convolution fusion | flops 1077936128 | bytes 17301504 | tf_op jit(solution)/shard_map/kab,kbc->kac/dot_general | solution.py:18
  31.9 2.0 %fusion.18 = f32[256,256]{1,0:T(8,128)S(1)} fusion(bf16[16,128,2048]{1,2,0:T(8,128)(2,1)} %convert_bitcast_fusion, bf16[16,128,2048]{1,2,0:T(8,128)(2,1)S(1)} %bitcast_multiply_fusion), kind=kOutput, calls=%fused_computation.16 | convolution fusion | flops 268500992 | bytes 2359296 | tf_op jit(solution)/shard_map/kbi,kbj->ij/dot_general | solution.py:28
  33.9 0.0 copy-start.2
  33.9 9.2 %collective-permute-start.1 = (f32[256,256]{1,0:T(8,128)S(1)}, f32[256,256]{1,0:T(8,128)S(1)}, u32[]{:S(2)}, u32[]{:S(2)}) collective-permute-start(f32[256,256]{1,0:T(8,128)S(1)} %fusion.18), channel_id=1, source_target_pairs={{0,32},{32,64},{64,96},{96,128},{128,160},{160,192},{192,224},{1,3... | collective-permute-start | bytes 786440 | tf_op jit(solution)/shard_map/ppermute | solution.py:14
  43.1 5.9 %bitcast_negate_fusion = f32[768,768]{1,0:T(8,128)} fusion(bf16[16,128,2048]{1,2,0:T(8,128)(2,1)} %convert_bitcast_fusion, bf16[16,128,2048]{1,2,0:T(8,128)(2,1)S(1)} %bitcast_multiply_fusion), kind=kOutput, calls=%fused_computation.8 | convolution fusion | flops 2416508928 | bytes 8650752 | tf_op jit(solution)/shard_map/kbi,kbj->ij/dot_general | solution.py:28
  49.1 1.9 %collective-permute-start = (f32[768,768]{1,0:T(8,128)}, f32[768,768]{1,0:T(8,128)}, u32[]{:S(2)}, u32[]{:S(2)}) collective-permute-start(f32[768,768]{1,0:T(8,128)} %bitcast_negate_fusion), channel_id=1, source_target_pairs={{0,1},{1,2},{2,3},{3,4},{4,5},{5,6},{6,7},{7,8},{8,9},{9,10},{10,1... | collective-permute-start | bytes 7077896 | tf_op jit(solution)/shard_map/ppermute | solution.py:14
  51.0 0.0 collective-permute-done.1
  51.0 0.0 copy-done.1
  51.0 2.4 %fusion.30 = (bf16[256,256]{1,0:T(8,128)(2,1)}, f32[256,256]{1,0:T(8,128)}) fusion(f32[256,256]{1,0:T(8,128)S(1)} %collective-permute-done.1, bf16[16,128,2048]{1,2,0:T(8,128)(2,1)} %convert_bitcast_fusion, bf16[16,128,2048]{1,2,0:T(8,128)(2,1)S(1)} %bitcast_multiply_fusion), kind=kOutput, calls=%fused_computation.30 | convolution fusion | flops 268632064 | bytes 2752512 | tf_op jit(solution)/shard_map/kbi,kbj->ij/dot_general | solution.py:28
  53.5 0.0 all-gather.2.cloned.1.call-update
  53.5 0.0 copy-done.2
  53.5 0.1 copy.20
  53.6 67.2 %all-gather.2.cloned.1.call-done = bf16[2048,256]{1,0:T(8,128)(2,1)} async-done(((bf16[256,256]{1,0:T(8,128)(2,1)}), bf16[2048,256]{1,0:T(8,128)(2,1)}) %all-gather.2.cloned.1.call-update) | async-done | bytes 1048592 | tf_op jit(solution)/shard_map/all_gather | solution.py:66
  120.8 2.4 %fusion.21 = f32[1,1,128,128]{3,2,1,0:T(8,128)} fusion(bf16[8,256,256]{2,1,0:T(8,128)(2,1)} %bitcast.57, bf16[128,8,256]{2,1,0:T(8,128)(2,1)S(1)} %bitcast.54), kind=kOutput, calls=%fused_computation.20 | convolution fusion | flops 201588736 | bytes 1638400 | tf_op jit(solution)/shard_map/rnl,snl->rs/dot_general | solution.py:73
  123.2 0.0 collective-permute-done
  123.2 7.6 %fusion.7 = f32[1,1,768,768]{3,2,1,0:T(8,128)} fusion(f32[768,768]{1,0:T(8,128)} %collective-permute-done, bf16[16,128,2048]{1,2,0:T(8,128)(2,1)} %convert_bitcast_fusion, bf16[16,128,2048]{1,2,0:T(8,128)(2,1)} %copy-done.1), kind=kOutput, calls=%fused_computation.11 | convolution fusion | flops 2417098752 | bytes 11010048 | tf_op jit(solution)/shard_map/kbi,kbj->ij/dot_general | solution.py:28
  (1 shorter events, 0.0 us)
Async XLA Ops:
  7.2 19.7 %copy-start = (bf16[1,1,16,128,128]{4,3,2,1,0:T(8,128)(2,1)S(1)}, bf16[1,1,16,128,128]{4,3,2,1,0:T(8,128)(2,1)}, u32[]{:S(2)}) copy-start(bf16[1,1,16,128,128]{4,3,2,1,0:T(8,128)(2,1)} %param.6) | copy-start | bytes 1572868
  7.2 13.1 %copy-start.3 = (s32[1,1,16,16]{3,2,1,0:T(8,128)S(1)}, s32[1,1,16,16]{3,2,1,0:T(8,128)}, u32[]{:S(2)}) copy-start(s32[1,1,16,16]{3,2,1,0:T(8,128)} %param.7) | copy-start | bytes 3076
  7.2 113.6 %all-gather.2.cloned.1.call-start = ((), (), s32[]{:S(2)}) async-start(), calls=%async_computation | async-start | bytes 1179648 | tf_op jit(solution)/shard_map/all_gather | solution.py:66
  26.8 24.2 %copy-start.1 = (bf16[16,128,2048]{1,2,0:T(8,128)(2,1)}, bf16[16,128,2048]{1,2,0:T(8,128)(2,1)S(1)}, u32[]{:S(2)}) copy-start(bf16[16,128,2048]{1,2,0:T(8,128)(2,1)S(1)} %bitcast_multiply_fusion) | copy-start | bytes 25165828
  33.9 19.6 %copy-start.2 = (bf16[1,1,128,2048]{3,2,1,0:T(8,128)(2,1)S(1)}, bf16[1,1,128,2048]{3,2,1,0:T(8,128)(2,1)}, u32[]{:S(2)}) copy-start(bf16[1,1,128,2048]{3,2,1,0:T(8,128)(2,1)} %param.9) | copy-start | bytes 1572868
  33.9 17.1 %collective-permute-start.1 = (f32[256,256]{1,0:T(8,128)S(1)}, f32[256,256]{1,0:T(8,128)S(1)}, u32[]{:S(2)}, u32[]{:S(2)}) collective-permute-start(f32[256,256]{1,0:T(8,128)S(1)} %fusion.18), channel_id=1, source_target_pairs={{0,32},{32,64},{64,96},{96,128},{128,160},{160,192},{192,224},{1,3... | collective-permute-start | bytes 786440 | tf_op jit(solution)/shard_map/ppermute | solution.py:14
  49.1 74.1 %collective-permute-start = (f32[768,768]{1,0:T(8,128)}, f32[768,768]{1,0:T(8,128)}, u32[]{:S(2)}, u32[]{:S(2)}) collective-permute-start(f32[768,768]{1,0:T(8,128)} %bitcast_negate_fusion), channel_id=1, source_target_pairs={{0,1},{1,2},{2,3},{3,4},{4,5},{5,6},{6,7},{7,8},{8,9},{9,10},{10,1... | collective-permute-start | bytes 7077896 | tf_op jit(solution)/shard_map/ppermute | solution.py:14
Sparse Core Ops, SparseCore 0:
  53.6 67.1 all-gather.1
where the time goes:
time: 138 us
  waiting for transfers between devices  67.2 us (49%)
  matrix products  25.4 us (18%)
  between operations  14.8 us (11%)
  local copies, waits for them, and re-layouts  12.6 us (9%)
  starting transfers between devices  11.2 us (8%)
  other arithmetic  6.46 us (5%)
    all_gather x1, waiting for transfers between devices, shards(): piece = lax.all_gather(front_half, 'ew', axis=0, tiled=True)  67.2 us
    dot_general x4, matrix products, edge_parts(): jnp.einsum('kbi,kbj->ij', slab, answer, preferred_element_type=jnp.float32)  17.9 us
    unnamed x10, local copies, waits for them, and re-layouts  12.5 us
    ppermute x2, starting transfers between devices, from_behind(): return lax.ppermute(block, axis, route)  11.2 us
    mul x1, other arithmetic, shards(): masked = coupling * keep[:, None, :]  6.38 us
    dot_general x1, matrix products, solve_all(): jnp.einsum('kab,kbc->kac', inverse, slabs, preferred_element_type=jnp.flo...  5.05 us
  transfers between devices with their start and end apart: 3, of which 1 were waited for; matrix products, arithmetic and copies ran while one was open for 8% of the time, Pallas kernels for 0%

commit v1 on v0

--- a/solution.py
+++ b/solution.py
@@ -63,7 +63,9 @@
     row_basis = basis[0, 0]
     rank = row_basis.shape[0]
     edge_width = SE * B
-    piece = lax.all_gather(front_half, "ew", axis=0, tiled=True)
+    piece = jnp.concatenate(
+        lax.all_to_all(jnp.stack([front_half] * lax.axis_size("ew")), "ew", 0, 0), axis=0
+    )
     pieces = piece.shape[0] // edge_width
     columns_here = row_basis.reshape(rank, pieces, edge_width)
     fronts = piece.reshape(pieces, edge_width, edge_width)

time: 138 us -> 109 us (0.79)
  the two profiles are of different devices: /device:TPU:2 before, /device:TPU:7 now
where the time goes in v1:
time: 109 us
  waiting for transfers between devices  44 us (40%)
  matrix products  24.1 us (22%)
  starting transfers between devices  19.2 us (18%)
  local copies, waits for them, and re-layouts  13.7 us (13%)
  other arithmetic  6.46 us (6%)
  between operations  1.41 us (1%)
    all_to_all x1, waiting for transfers between devices, shards(): lax.all_to_all(jnp.stack([front_half] * lax.axis_size('ew')), 'ew', 0, 0)  44 us
    dot_general x4, matrix products, edge_parts(): jnp.einsum('kbi,kbj->ij', slab, answer, preferred_element_type=jnp.float32)  17.9 us
    unnamed x10, local copies, waits for them, and re-layouts  12.5 us
    ppermute x2, starting transfers between devices, from_behind(): return lax.ppermute(block, axis, route)  12.3 us
    all_to_all x1, starting transfers between devices, shards(): lax.all_to_all(jnp.stack([front_half] * lax.axis_size('ew')), 'ew', 0, 0)  6.8 us
    mul x1, other arithmetic, shards(): masked = coupling * keep[:, None, :]  6.38 us
    dot_general x1, matrix products, solve_all(): jnp.einsum('kab,kbc->kac', inverse, slabs, preferred_element_type=jnp.flo...  5.06 us
  transfers between devices with their start and end apart: 3, of which 1 were waited for; matrix products, arithmetic and copies ran while one was open for 10% of the time, Pallas kernels for 0%

profile of v1, /device:TPU:7, one launch (start us, length us, event | category | flops | bytes accessed | tf_op | source)
XLA Modules:
  0.0 108.8 jit_solution(7335699066726274290)
XLA Ops:
  0.6 0.0 copy-start
  0.6 0.0 copy-start.3
  0.7 12.4 %copy.8 = bf16[1,1,16,128,2048]{3,4,2,1,0:T(8,128)(2,1)} copy(bf16[1,1,16,128,2048]{4,3,2,1,0:T(8,128)(2,1)} %param.5) | data formatting | bytes 16777216 | tf_op args[0]
  13.7 0.0 copy-done.3
  13.7 0.1 broadcast_in_dim.14
  13.8 0.1 fusion.29
  13.9 6.4 %bitcast_multiply_fusion = bf16[16,128,2048]{1,2,0:T(8,128)(2,1)S(1)} fusion(bf16[1,1,16,128,2048]{3,4,2,1,0:T(8,128)(2,1)} %copy.8, bf16[16,2048]{1,0:T(8,128)(2,1)S(1)} %fusion.29), kind=kLoop, calls=%fused_computation | loop fusion | flops 4194304 | bytes 16842752 | tf_op jit(solution)/shard_map/mul | solution.py:54
  20.3 0.0 copy-done
  20.3 0.0 copy-start.1
  20.3 5.1 %convert_bitcast_fusion = bf16[16,128,2048]{1,2,0:T(8,128)(2,1)} fusion(bf16[16,128,2048]{1,2,0:T(8,128)(2,1)S(1)} %bitcast_multiply_fusion, bf16[1,1,16,128,128]{4,3,2,1,0:T(8,128)(2,1)S(1)} %copy-done), kind=kOutput, calls=%fused_computation.1 | convolution fusion | flops 1077936128 | bytes 17301504 | tf_op jit(solution)/shard_map/kab,kbc->kac/dot_general | solution.py:18
  25.4 2.0 %fusion.18 = f32[256,256]{1,0:T(8,128)S(1)} fusion(bf16[16,128,2048]{1,2,0:T(8,128)(2,1)} %convert_bitcast_fusion, bf16[16,128,2048]{1,2,0:T(8,128)(2,1)S(1)} %bitcast_multiply_fusion), kind=kOutput, calls=%fused_computation.16 | convolution fusion | flops 268500992 | bytes 2359296 | tf_op jit(solution)/shard_map/kbi,kbj->ij/dot_general | solution.py:28
  27.3 0.0 copy-start.2
  27.3 9.0 %collective-permute-start.1 = (f32[256,256]{1,0:T(8,128)S(1)}, f32[256,256]{1,0:T(8,128)S(1)}, u32[]{:S(2)}, u32[]{:S(2)}) collective-permute-start(f32[256,256]{1,0:T(8,128)S(1)} %fusion.18), channel_id=1, source_target_pairs={{0,32},{32,64},{64,96},{96,128},{128,160},{160,192},{192,224},{1,3... | collective-permute-start | bytes 786440 | tf_op jit(solution)/shard_map/ppermute | solution.py:14
  36.3 5.9 %bitcast_negate_fusion = f32[768,768]{1,0:T(8,128)} fusion(bf16[16,128,2048]{1,2,0:T(8,128)(2,1)} %convert_bitcast_fusion, bf16[16,128,2048]{1,2,0:T(8,128)(2,1)S(1)} %bitcast_multiply_fusion), kind=kOutput, calls=%fused_computation.8 | convolution fusion | flops 2416508928 | bytes 8650752 | tf_op jit(solution)/shard_map/kbi,kbj->ij/dot_general | solution.py:28
  42.2 3.4 %collective-permute-start = (f32[768,768]{1,0:T(8,128)}, f32[768,768]{1,0:T(8,128)}, u32[]{:S(2)}, u32[]{:S(2)}) collective-permute-start(f32[768,768]{1,0:T(8,128)} %bitcast_negate_fusion), channel_id=1, source_target_pairs={{0,1},{1,2},{2,3},{3,4},{4,5},{5,6},{6,7},{7,8},{8,9},{9,10},{10,1... | collective-permute-start | bytes 7077896 | tf_op jit(solution)/shard_map/ppermute | solution.py:14
  45.6 0.0 collective-permute-done.1
  45.7 0.0 copy-done.1
  45.7 2.4 %fusion.30 = (bf16[256,256]{1,0:T(8,128)(2,1)S(1)}, f32[256,256]{1,0:T(8,128)}) fusion(f32[256,256]{1,0:T(8,128)S(1)} %collective-permute-done.1, bf16[16,128,2048]{1,2,0:T(8,128)(2,1)} %convert_bitcast_fusion, bf16[16,128,2048]{1,2,0:T(8,128)(2,1)S(1)} %bitcast_multiply_fusion), kind=kOutput, calls=%fused_computation.30 | convolution fusion | flops 268632064 | bytes 2752512 | tf_op jit(solution)/shard_map/kbi,kbj->ij/dot_general | solution.py:28
  48.1 1.1 stack.2
  49.1 6.8 %all-to-all-start = ((bf16[8,256,256]{2,1,0:T(8,128)(2,1)}), bf16[8,256,256]{2,1,0:T(8,128)(2,1)S(1)}, u32[]{:S(2)}, u32[]{:S(2)}) async-start(bf16[8,256,256]{2,1,0:T(8,128)(2,1)} %stack.2), calls=%async_computation | async-start | bytes 2097152 | tf_op jit(solution)/shard_map/all_to_all | solution.py:67
  56.0 0.0 copy-done.2
  56.0 0.1 copy.20
  56.1 44.0 %all-to-all-done = bf16[8,256,256]{2,1,0:T(8,128)(2,1)S(1)} async-done(((bf16[8,256,256]{2,1,0:T(8,128)(2,1)}), bf16[8,256,256]{2,1,0:T(8,128)(2,1)S(1)}, u32[]{:S(2)}, u32[]{:S(2)}) %all-to-all-start) | async-done | bytes 1048608 | tf_op jit(solution)/shard_map/all_to_all | solution.py:67
  100.1 1.2 %fusion.21 = f32[1,1,128,128]{3,2,1,0:T(8,128)} fusion(bf16[8,256,256]{2,1,0:T(8,128)(2,1)S(1)} %all-to-all-done, bf16[128,8,256]{2,1,0:T(8,128)(2,1)S(1)} %bitcast.53), kind=kOutput, calls=%fused_computation.20 | convolution fusion | flops 201588736 | bytes 1638400 | tf_op jit(solution)/shard_map/rnl,snl->rs/dot_general | solution.py:75
  101.2 0.0 collective-permute-done
  101.2 7.6 %fusion.7 = f32[1,1,768,768]{3,2,1,0:T(8,128)} fusion(f32[768,768]{1,0:T(8,128)} %collective-permute-done, bf16[16,128,2048]{1,2,0:T(8,128)(2,1)} %convert_bitcast_fusion, bf16[16,128,2048]{1,2,0:T(8,128)(2,1)} %copy-done.1), kind=kOutput, calls=%fused_computation.11 | convolution fusion | flops 2417098752 | bytes 11010048 | tf_op jit(solution)/shard_map/kbi,kbj->ij/dot_general | solution.py:28
  (1 shorter events, 0.0 us)
Async XLA Ops:
  0.6 19.6 %copy-start = (bf16[1,1,16,128,128]{4,3,2,1,0:T(8,128)(2,1)S(1)}, bf16[1,1,16,128,128]{4,3,2,1,0:T(8,128)(2,1)}, u32[]{:S(2)}) copy-start(bf16[1,1,16,128,128]{4,3,2,1,0:T(8,128)(2,1)} %param.6) | copy-start | bytes 1572868
  0.6 13.1 %copy-start.3 = (s32[1,1,16,16]{3,2,1,0:T(8,128)S(1)}, s32[1,1,16,16]{3,2,1,0:T(8,128)}, u32[]{:S(2)}) copy-start(s32[1,1,16,16]{3,2,1,0:T(8,128)} %param.7) | copy-start | bytes 3076
  20.3 25.4 %copy-start.1 = (bf16[16,128,2048]{1,2,0:T(8,128)(2,1)}, bf16[16,128,2048]{1,2,0:T(8,128)(2,1)S(1)}, u32[]{:S(2)}) copy-start(bf16[16,128,2048]{1,2,0:T(8,128)(2,1)S(1)} %bitcast_multiply_fusion) | copy-start | bytes 25165828
  27.3 28.6 %copy-start.2 = (bf16[1,1,128,2048]{3,2,1,0:T(8,128)(2,1)S(1)}, bf16[1,1,128,2048]{3,2,1,0:T(8,128)(2,1)}, u32[]{:S(2)}) copy-start(bf16[1,1,128,2048]{3,2,1,0:T(8,128)(2,1)} %param.9) | copy-start | bytes 1572868
  27.3 18.3 %collective-permute-start.1 = (f32[256,256]{1,0:T(8,128)S(1)}, f32[256,256]{1,0:T(8,128)S(1)}, u32[]{:S(2)}, u32[]{:S(2)}) collective-permute-start(f32[256,256]{1,0:T(8,128)S(1)} %fusion.18), channel_id=1, source_target_pairs={{0,32},{32,64},{64,96},{96,128},{128,160},{160,192},{192,224},{1,3... | collective-permute-start | bytes 786440 | tf_op jit(solution)/shard_map/ppermute | solution.py:14
  42.2 59.0 %collective-permute-start = (f32[768,768]{1,0:T(8,128)}, f32[768,768]{1,0:T(8,128)}, u32[]{:S(2)}, u32[]{:S(2)}) collective-permute-start(f32[768,768]{1,0:T(8,128)} %bitcast_negate_fusion), channel_id=1, source_target_pairs={{0,1},{1,2},{2,3},{3,4},{4,5},{5,6},{6,7},{7,8},{8,9},{9,10},{10,1... | collective-permute-start | bytes 7077896 | tf_op jit(solution)/shard_map/ppermute | solution.py:14
  49.1 50.9 %all-to-all-start = ((bf16[8,256,256]{2,1,0:T(8,128)(2,1)}), bf16[8,256,256]{2,1,0:T(8,128)(2,1)S(1)}, u32[]{:S(2)}, u32[]{:S(2)}) async-start(bf16[8,256,256]{2,1,0:T(8,128)(2,1)} %stack.2), calls=%async_computation | async-start | bytes 2097152 | tf_op jit(solution)/shard_map/all_to_all | solution.py:67
